TPU v7x, 256 devices: a whole 4x4x8 slice. The times are simulated.
256 devices in a mesh: corner: 16 (over y, x_lo, core), tm: 16 (over z, x_hi).
Axes of the slice: x: 4 (x_hi: 2, x_lo: 2; x = x_hi * 2 + x_lo), y: 4, z: 8, core: 2. Of those that a mesh axis runs over, the one named last changes fastest.
Arguments:
- signal: bfloat16 [16, 64, 65536], P('corner', None, 'tm'), may hold values from -6 to 6
- dilated_conv_weight: bfloat16 [2, 256, 128], replicated, may hold values from -0.5 to 0.5
- dilated_conv_bias: float32 [2, 256], replicated, may hold values from -3 to 3
- projection_weight: bfloat16 [2, 128, 128], replicated, may hold values from -0.5 to 0.5
- projection_bias: float32 [2, 128], replicated, may hold values from -3 to 3
- cot_top: bfloat16 [16, 64, 65536], P('corner', None, 'tm'), may hold values from -6 to 6
- cot_skip: bfloat16 [16, 64, 65536], P('corner', None, 'tm'), may hold values from -6 to 6
Outputs:
- x_top: bfloat16 [16, 64, 65536], P('corner', None, 'tm')
- skip_sum: bfloat16 [16, 64, 65536], P('corner', None, 'tm')
- grad_input: bfloat16 [16, 64, 65536], P('corner', None, 'tm')
- grad_conv: float32 [2, 256, 128], replicated
- grad_conv_bias: float32 [2, 256], replicated
- grad_out: float32 [2, 128, 128], replicated
- grad_out_bias: float32 [2, 128], replicated
All inputs are finite; a program needn't handle non-finite values.
Results may differ from a plain program's by a relative error of at most 0.0065.
Values may be sent and summed in bfloat16 or wider, within the bound.
No kernel may reach another device: no remote copies, remote signals or barrier semaphores. Data moves between devices by JAX's collectives and lax.ppermute only.
A program may use at most 64 MiB of HBM per device.

v0:
```python
import math
import jax
import jax.numpy as jnp
from jax import lax
from jax.sharding import PartitionSpec as P


def from_behind(block, axis, distance):
    devices = range(lax.axis_size(axis))
    route = [(i - distance, i) for i in devices if i - distance in devices]
    return lax.ppermute(block, axis, route)


def gated_layer_forward(a_in, tap_in, weight, bias, proj, proj_bias, gsize, rsize):
    stacked = jnp.concatenate([tap_in, a_in], axis=1)
    pre_act = (
        jnp.einsum("oc,bct->bot", weight, stacked, preferred_element_type=jnp.float32)
        + bias[None, :, None]
    )
    gate_out = (jnp.tanh(pre_act[:, :gsize]) * jax.nn.sigmoid(pre_act[:, gsize:])).astype(
        jnp.bfloat16
    )
    mixed = (
        jnp.einsum("og,bgt->bot", proj, gate_out, preferred_element_type=jnp.float32)
        + proj_bias[None, :, None]
    )
    next_act = (a_in.astype(jnp.float32) + mixed[:, :rsize]).astype(jnp.bfloat16)
    return (stacked, pre_act, gate_out, next_act, mixed[:, rsize:])


def layer_backward(go_res, go_skip, stacked, pre_act, gate_out, weight, proj, gsize, rsize):
    upper = jnp.concatenate([go_res, go_skip], axis=1)
    grad_proj = jnp.einsum("bot,bgt->og", upper, gate_out, preferred_element_type=jnp.float32)
    grad_pbias = jnp.sum(upper, axis=(0, 2), dtype=jnp.float32)
    grad_gate = jnp.einsum("og,bot->bgt", proj, upper, preferred_element_type=jnp.float32)
    filt_act = jnp.tanh(pre_act[:, :gsize])
    gate_act = jax.nn.sigmoid(pre_act[:, gsize:])
    grad_pre = jnp.concatenate(
        [
            grad_gate * gate_act * (1.0 - filt_act * filt_act),
            grad_gate * filt_act * gate_act * (1.0 - gate_act),
        ],
        axis=1,
    ).astype(jnp.bfloat16)
    grad_weight = jnp.einsum("bot,bct->oc", grad_pre, stacked, preferred_element_type=jnp.float32)
    grad_bias = jnp.sum(grad_pre, axis=(0, 2), dtype=jnp.float32)
    grad_in = jnp.einsum("oc,bot->bct", weight, grad_pre, preferred_element_type=jnp.float32)
    return (
        grad_in[:, :rsize].astype(jnp.bfloat16),
        grad_in[:, rsize:],
        (grad_weight, grad_bias, grad_proj, grad_pbias),
    )


def on_device(
    signal,
    dilated_conv_weight,
    dilated_conv_bias,
    projection_weight,
    projection_bias,
    cot_top,
    cot_skip,
):
    rsize = signal.shape[1]
    gsize = projection_weight.shape[2]
    tap_near = from_behind(signal, "tm", 1)
    (
        lower_saved_state,
        lower_preactivation,
        lower_gated_output,
        middle_layer_input,
        lower_skip_output,
    ) = gated_layer_forward(
        signal,
        tap_near,
        dilated_conv_weight[0],
        dilated_conv_bias[0],
        projection_weight[0],
        projection_bias[0],
        gsize,
        rsize,
    )
    tap_far = from_behind(middle_layer_input, "tm", 2)
    (
        upper_saved_state,
        upper_preactivation,
        upper_gated_output,
        upper_layer_output,
        upper_skip_output,
    ) = gated_layer_forward(
        middle_layer_input,
        tap_far,
        dilated_conv_weight[1],
        dilated_conv_bias[1],
        projection_weight[1],
        projection_bias[1],
        gsize,
        rsize,
    )
    skip_out = (lower_skip_output + upper_skip_output).astype(jnp.bfloat16)
    delayed_gradient_upper, current_gradient_upper, grads_top = layer_backward(
        cot_top,
        cot_skip,
        upper_saved_state,
        upper_preactivation,
        upper_gated_output,
        dilated_conv_weight[1],
        projection_weight[1],
        gsize,
        rsize,
    )
    later_top = from_behind(delayed_gradient_upper, "tm", -2)
    middle_input_gradient = (
        cot_top.astype(jnp.float32) + current_gradient_upper + later_top.astype(jnp.float32)
    ).astype(jnp.bfloat16)
    delayed_gradient_lower, current_gradient_lower, grads_low = layer_backward(
        middle_input_gradient,
        cot_skip,
        lower_saved_state,
        lower_preactivation,
        lower_gated_output,
        dilated_conv_weight[0],
        projection_weight[0],
        gsize,
        rsize,
    )
    later_low = from_behind(delayed_gradient_lower, "tm", -1)
    lower_input_gradient = (
        middle_input_gradient.astype(jnp.float32)
        + current_gradient_lower
        + later_low.astype(jnp.float32)
    ).astype(jnp.bfloat16)
    summed = lax.psum(
        (
            jnp.stack([grads_low[0], grads_top[0]]),
            jnp.stack([grads_low[1], grads_top[1]]),
            jnp.stack([grads_low[2], grads_top[2]]),
            jnp.stack([grads_low[3], grads_top[3]]),
        ),
        ("corner", "tm"),
    )
    count = signal.shape[0] * lax.axis_size("corner") * signal.shape[2] * lax.axis_size("tm")
    scale = 1.0 / math.sqrt(count)
    return (
        upper_layer_output,
        skip_out,
        lower_input_gradient,
        summed[0] * scale,
        summed[1] * scale,
        summed[2] * scale,
        summed[3] * scale,
    )


def solution(mesh):
    return jax.shard_map(
        on_device,
        mesh=mesh,
        in_specs=(
            P("corner", None, "tm"),
            P(),
            P(),
            P(),
            P(),
            P("corner", None, "tm"),
            P("corner", None, "tm"),
        ),
        out_specs=(
            P("corner", None, "tm"),
            P("corner", None, "tm"),
            P("corner", None, "tm"),
            P(),
            P(),
            P(),
            P(),
        ),
        check_vma=False,
    )
```

profile of v0, /device:TPU:1, one launch (start us, length us, event | category | flops | bytes accessed | tf_op | source)
XLA Modules:
  0.0 411.1 jit_solution(4979422311224916654)
XLA Ops:
  7.2 5.5 %collective-permute-start = (bf16[1,64,4096]{2,1,0:T(8,128)(2,1)}, bf16[1,64,4096]{2,1,0:T(8,128)(2,1)S(1)}, u32[]{:S(2)}, u32[]{:S(2)}) collective-permute-start(bf16[1,64,4096]{2,1,0:T(8,128)(2,1)} %param.7), channel_id=1, source_target_pairs={{0,1},{1,2},{2,3},{3,4},{4,5},{5,6},{6,7},{7,8},{8,9},{9,10},{10,1... | collective-permute-start | bytes 1572872 | tf_op jit(solution)/shard_map/ppermute | solution.py:11
  12.7 0.8 fusion.55
  13.5 0.8 slice_bitcast_fusion
  14.2 1.1 constant_dynamic-update-slice_fusion.1
  15.3 8.3 %collective-permute-done = bf16[1,64,4096]{2,1,0:T(8,128)(2,1)S(1)} collective-permute-done((bf16[1,64,4096]{2,1,0:T(8,128)(2,1)}, bf16[1,64,4096]{2,1,0:T(8,128)(2,1)S(1)}, u32[]{:S(2)}, u32[]{:S(2)}) %collective-permute-start) | collective-permute-done | bytes 524320 | tf_op jit(solution)/shard_map/ppermute | solution.py:11
  23.6 2.0 fusion.1
  25.6 0.8 fusion.18
  26.9 0.6 copy-done.6
  27.6 5.3 %collective-permute-start.1 = (bf16[1,64,4096]{2,1,0:T(8,128)(2,1)S(1)}, bf16[1,64,4096]{2,1,0:T(8,128)(2,1)S(1)}, u32[]{:S(2)}, u32[]{:S(2)}) collective-permute-start(bf16[1,64,4096]{2,1,0:T(8,128)(2,1)S(1)} %fusion.26), channel_id=1, source_target_pairs={{0,2},{1,3},{2,4},{3,5},{4,6},{5,7},{6,8},{7,9},{8,10},{9,11},{10,... | collective-permute-start | bytes 1572872 | tf_op jit(solution)/shard_map/ppermute | solution.py:11
  33.2 9.3 %collective-permute-done.1 = bf16[1,64,4096]{2,1,0:T(8,128)(2,1)S(1)} collective-permute-done((bf16[1,64,4096]{2,1,0:T(8,128)(2,1)S(1)}, bf16[1,64,4096]{2,1,0:T(8,128)(2,1)S(1)}, u32[]{:S(2)}, u32[]{:S(2)}) %collective-permute-start.1) | collective-permute-done | bytes 524320 | tf_op jit(solution)/shard_map/ppermute | solution.py:11
  42.5 0.7 fusion.3
  43.3 1.5 multiply_convert_fusion.3
  44.8 0.5 convolution_bitcast_fusion.6
  45.3 1.3 collective-permute-start.2
  47.0 1.2 fusion.24
  48.6 0.7 fusion.16
  49.3 0.4 convolution_bitcast_fusion.8
  49.8 9.4 %collective-permute-done.2 = bf16[1,64,4096]{2,1,0:T(8,128)(2,1)S(1)} collective-permute-done((bf16[1,64,4096]{2,1,0:T(8,128)(2,1)S(1)}, bf16[1,64,4096]{2,1,0:T(8,128)(2,1)S(1)}, u32[]{:S(2)}, u32[]{:S(2)}) %collective-permute-start.2) | collective-permute-done | bytes 524320 | tf_op jit(solution)/shard_map/ppermute | solution.py:11
  59.3 1.3 multiply_convert_fusion.1
  62.0 82.7 %all-reduce = (f32[2,256]{1,0:T(2,128)S(1)}, f32[2,128]{1,0:T(2,128)S(1)}) all-reduce(f32[2,256]{1,0:T(2,128)S(1)} %pad_maximum_fusion.15, f32[2,128]{1,0:T(2,128)S(1)} %pad_maximum_fusion.16), channel_id=1, replica_groups=mesh['corner'=16,'tm'=16] {'corner','tm'}, use_global_device_ids=true, to_apply=%region_3.0 | all-reduce | flops 768 | bytes 6144 | tf_op jit(solution)/shard_map/psum | solution.py:133
  144.7 0.6 broadcast_multiply_fusion.2
  145.3 2.2 convolution_bitcast_fusion.4
  147.5 0.8 slice.202
  148.3 1.3 collective-permute-start.3
  149.6 0.7 pad_maximum_fusion.14
  150.3 0.7 fusion.17
  151.0 0.7 pad_maximum_fusion.13
  151.7 0.6 broadcast_multiply_fusion.3
  152.3 246.7 %all-reduce.4.cloned.1.call-done = (f32[2,256,128]{2,1,0:T(8,128)}, f32[2,128,128]{2,1,0:T(8,128)}) async-done(((f32[2,256,128]{2,1,0:T(8,128)}, f32[2,128,128]{2,1,0:T(8,128)}), (f32[2,256,128]{2,1,0:T(8,128)}, f32[2,128,128]{2,1,0:T(8,128)})) %all-reduce.4.cloned.1.call-update) | async-done | bytes 393232 | tf_op jit(solution)/shard_map/psum | solution.py:133
  399.0 1.6 broadcast_multiply_fusion.1
  400.6 1.7 broadcast_multiply_fusion
  402.2 2.0 fusion.21
  (37 shorter events, 3.2 us)
Async XLA Ops:
  7.2 391.8 %all-reduce.4.cloned.1.call-start = ((), (), s32[]{:S(2)}) async-start(), calls=%async_computation | async-start | bytes 786432 | tf_op jit(solution)/shard_map/psum | solution.py:133
  7.2 16.4 %collective-permute-start = (bf16[1,64,4096]{2,1,0:T(8,128)(2,1)}, bf16[1,64,4096]{2,1,0:T(8,128)(2,1)S(1)}, u32[]{:S(2)}, u32[]{:S(2)}) collective-permute-start(bf16[1,64,4096]{2,1,0:T(8,128)(2,1)} %param.7), channel_id=1, source_target_pairs={{0,1},{1,2},{2,3},{3,4},{4,5},{5,6},{6,7},{7,8},{8,9},{9,10},{10,1... | collective-permute-start | bytes 1572872 | tf_op jit(solution)/shard_map/ppermute | solution.py:11
  23.6 2.0 copy-start.8
  25.6 0.9 copy-start.10
  26.4 1.0 copy-start.6
  26.4 6.5 %copy-start.5 = (bf16[1,64,4096]{2,1,0:T(8,128)(2,1)S(1)}, bf16[1,64,4096]{2,1,0:T(8,128)(2,1)}, u32[]{:S(2)}) copy-start(bf16[1,64,4096]{2,1,0:T(8,128)(2,1)} %param.13) | copy-start | bytes 1572868
  27.5 15.1 %copy-start.7 = (bf16[2,256,128]{2,1,0:T(8,128)(2,1)S(1)}, bf16[2,256,128]{2,1,0:T(8,128)(2,1)}, u32[]{:S(2)}) copy-start(bf16[2,256,128]{2,1,0:T(8,128)(2,1)} %param.8) | copy-start | bytes 393220
  27.6 15.0 %collective-permute-start.1 = (bf16[1,64,4096]{2,1,0:T(8,128)(2,1)S(1)}, bf16[1,64,4096]{2,1,0:T(8,128)(2,1)S(1)}, u32[]{:S(2)}, u32[]{:S(2)}) collective-permute-start(bf16[1,64,4096]{2,1,0:T(8,128)(2,1)S(1)} %fusion.26), channel_id=1, source_target_pairs={{0,2},{1,3},{2,4},{3,5},{4,6},{5,7},{6,8},{7,9},{8,10},{9,11},{10,... | collective-permute-start | bytes 1572872 | tf_op jit(solution)/shard_map/ppermute | solution.py:11
  45.3 13.9 %collective-permute-start.2 = (bf16[1,64,4096]{2,1,0:T(8,128)(2,1)S(1)}, bf16[1,64,4096]{2,1,0:T(8,128)(2,1)S(1)}, u32[]{:S(2)}, u32[]{:S(2)}) collective-permute-start(bf16[1,64,4096]{2,1,0:T(8,128)(2,1)S(1)} %slice.203), channel_id=1, source_target_pairs={{2,0},{3,1},{4,2},{5,3},{6,4},{7,5},{8,6},{9,7},{10,8},{11,9},{12,... | collective-permute-start | bytes 1572872 | tf_op jit(solution)/shard_map/ppermute | solution.py:11
  49.3 9.8 %copy-start.4 = (bf16[1,64,4096]{2,1,0:T(8,128)(2,1)S(1)}, bf16[1,64,4096]{2,1,0:T(8,128)(2,1)}, u32[]{:S(2)}) copy-start(bf16[1,64,4096]{2,1,0:T(8,128)(2,1)} %param.12) | copy-start | bytes 1572868
  60.7 1.1 copy-start
  60.7 1.3 copy-start.2
  145.3 5.0 %copy-start.1 = (bf16[1,128,4096]{2,1,0:T(8,128)(2,1)S(1)}, bf16[1,128,4096]{2,1,0:T(8,128)(2,1)}, u32[]{:S(2)}) copy-start(bf16[1,128,4096]{2,1,0:T(8,128)(2,1)} %copy-done) | copy-start | bytes 3145732
  145.3 5.0 %copy-start.3 = (bf16[1,128,4096]{2,1,0:T(8,128)(2,1)S(1)}, bf16[1,128,4096]{2,1,0:T(8,128)(2,1)}, u32[]{:S(2)}) copy-start(bf16[1,128,4096]{2,1,0:T(8,128)(2,1)} %copy-done.2) | copy-start | bytes 3145732
  145.3 5.0 %copy-start.9 = (bf16[1,64,4096]{2,1,0:T(8,128)(2,1)S(1)}, bf16[1,64,4096]{2,1,0:T(8,128)(2,1)}, u32[]{:S(2)}) copy-start(bf16[1,64,4096]{2,1,0:T(8,128)(2,1)} %copy-done.8) | copy-start | bytes 1572868
  148.3 253.9 %collective-permute-start.3 = (bf16[1,64,4096]{2,1,0:T(8,128)(2,1)}, bf16[1,64,4096]{2,1,0:T(8,128)(2,1)}, u32[]{:S(2)}, u32[]{:S(2)}) collective-permute-start(bf16[1,64,4096]{2,1,0:T(8,128)(2,1)} %slice.202), channel_id=1, source_target_pairs={{1,0},{2,1},{3,2},{4,3},{5,4},{6,5},{7,6},{8,7},{9,8},{10,9},{11,1... | collective-permute-start | bytes 1572872 | tf_op jit(solution)/shard_map/ppermute | solution.py:11
Sparse Core Ops, SparseCore 0:
  151.9 247.0 all-reduce.3
where the time goes:
time: 412 us; the launch traced here: 411 us
  waiting for transfers between devices  274 us (67%)
  blocking collectives  82.7 us (20%)
  between operations  14.3 us (3%)
  starting transfers between devices  13.5 us (3%)
  matrix products  11.3 us (3%)
  other arithmetic  11.3 us (3%)
  local copies, waits for them, and re-layouts  4.41 us (1%)
    psum x1, waiting for transfers between devices, on_device(): lax.psum((jnp.stack([grads_low[0], grads_top[0]]), jnp.stack([grads_low[1...  247 us
    psum x1, blocking collectives, on_device(): lax.psum((jnp.stack([grads_low[0], grads_top[0]]), jnp.stack([grads_low[1...  82.7 us
    ppermute x4, waiting for transfers between devices, from_behind(): return lax.ppermute(block, axis, route)  27 us
    ppermute x4, starting transfers between devices, from_behind(): return lax.ppermute(block, axis, route)  13.4 us
  transfers between devices with their start and end apart: 5, of which 4 were waited for; matrix products, arithmetic and copies ran while one was open for 3% of the time, Pallas kernels for 0%

commit v1 on v0

--- a/solution.py
+++ b/solution.py
@@ -131,13 +131,16 @@
         + later_low.astype(jnp.float32)
     ).astype(jnp.bfloat16)
     summed = lax.psum(
-        (
-            jnp.stack([grads_low[0], grads_top[0]]),
-            jnp.stack([grads_low[1], grads_top[1]]),
-            jnp.stack([grads_low[2], grads_top[2]]),
-            jnp.stack([grads_low[3], grads_top[3]]),
+        lax.psum(
+            (
+                jnp.stack([grads_low[0], grads_top[0]]),
+                jnp.stack([grads_low[1], grads_top[1]]),
+                jnp.stack([grads_low[2], grads_top[2]]),
+                jnp.stack([grads_low[3], grads_top[3]]),
+            ),
+            "corner",
         ),
-        ("corner", "tm"),
+        "tm",
     )
     count = signal.shape[0] * lax.axis_size("corner") * signal.shape[2] * lax.axis_size("tm")
     scale = 1.0 / math.sqrt(count)

time: 412 us -> 370 us (0.90)
  the two profiles are of different devices: /device:TPU:1 before, /device:TPU:8 now
where the time goes in v1:
time: 370 us
  waiting for transfers between devices  247 us (67%)
  blocking collectives  70.9 us (19%)
  between operations  14.3 us (4%)
  starting transfers between devices  13.2 us (4%)
  other arithmetic  10.2 us (3%)
  matrix products  9.4 us (3%)
  local copies, waits for them, and re-layouts  4.14 us (1%)
    psum x1, waiting for transfers between devices, on_device(): lax.psum(lax.psum((jnp.stack([grads_low[0], grads_top[0]]), jnp.stack([gr...  166 us
    psum x1, waiting for transfers between devices, on_device(): lax.psum((jnp.stack([grads_low[0], grads_top[0]]), jnp.stack([grads_low[1...  52.6 us
    psum x1, blocking collectives, on_device(): lax.psum(lax.psum((jnp.stack([grads_low[0], grads_top[0]]), jnp.stack([gr...  43.6 us
    ppermute x4, waiting for transfers between devices, from_behind(): return lax.ppermute(block, axis, route)  28.9 us
    psum x1, blocking collectives, on_device(): lax.psum((jnp.stack([grads_low[0], grads_top[0]]), jnp.stack([grads_low[1...  27.3 us
    ppermute x4, starting transfers between devices, from_behind(): return lax.ppermute(block, axis, route)  13.1 us
  transfers between devices with their start and end apart: 6, of which 5 were waited for; matrix products, arithmetic and copies ran while one was open for 3% of the time, Pallas kernels for 0%

profile of v1, /device:TPU:8, one launch (start us, length us, event | category | flops | bytes accessed | tf_op | source)
XLA Modules:
  0.0 369.6 jit_solution(15206140490801051141)
XLA Ops:
  7.2 5.0 %collective-permute-start = (bf16[1,64,4096]{2,1,0:T(8,128)(2,1)}, bf16[1,64,4096]{2,1,0:T(8,128)(2,1)S(1)}, u32[]{:S(2)}, u32[]{:S(2)}) collective-permute-start(bf16[1,64,4096]{2,1,0:T(8,128)(2,1)} %param.7), channel_id=1, source_target_pairs={{0,1},{1,2},{2,3},{3,4},{4,5},{5,6},{6,7},{7,8},{8,9},{9,10},{10,1... | collective-permute-start | bytes 1572872 | tf_op jit(solution)/shard_map/ppermute | solution.py:11
  12.2 0.8 fusion.55
  12.9 0.8 slice_bitcast_fusion
  13.7 1.1 constant_dynamic-update-slice_fusion.1
  14.8 8.8 %collective-permute-done = bf16[1,64,4096]{2,1,0:T(8,128)(2,1)S(1)} collective-permute-done((bf16[1,64,4096]{2,1,0:T(8,128)(2,1)}, bf16[1,64,4096]{2,1,0:T(8,128)(2,1)S(1)}, u32[]{:S(2)}, u32[]{:S(2)}) %collective-permute-start) | collective-permute-done | bytes 524320 | tf_op jit(solution)/shard_map/ppermute | solution.py:11
  23.6 1.8 fusion.1
  25.4 0.8 fusion.18
  26.7 0.6 copy-done.2
  27.4 5.6 %collective-permute-start.1 = (bf16[1,64,4096]{2,1,0:T(8,128)(2,1)S(1)}, bf16[1,64,4096]{2,1,0:T(8,128)(2,1)S(1)}, u32[]{:S(2)}, u32[]{:S(2)}) collective-permute-start(bf16[1,64,4096]{2,1,0:T(8,128)(2,1)S(1)} %fusion.26), channel_id=1, source_target_pairs={{0,2},{1,3},{2,4},{3,5},{4,6},{5,7},{6,8},{7,9},{8,10},{9,11},{10,... | collective-permute-start | bytes 1572872 | tf_op jit(solution)/shard_map/ppermute | solution.py:11
  33.3 10.0 %collective-permute-done.1 = bf16[1,64,4096]{2,1,0:T(8,128)(2,1)S(1)} collective-permute-done((bf16[1,64,4096]{2,1,0:T(8,128)(2,1)S(1)}, bf16[1,64,4096]{2,1,0:T(8,128)(2,1)S(1)}, u32[]{:S(2)}, u32[]{:S(2)}) %collective-permute-start.1) | collective-permute-done | bytes 524320 | tf_op jit(solution)/shard_map/ppermute | solution.py:11
  43.3 0.7 fusion.3
  44.0 1.5 multiply_convert_fusion.3
  46.0 1.3 collective-permute-start.2
  47.8 1.2 fusion.24
  49.3 0.7 fusion.16
  50.5 10.1 %collective-permute-done.2 = bf16[1,64,4096]{2,1,0:T(8,128)(2,1)S(1)} collective-permute-done((bf16[1,64,4096]{2,1,0:T(8,128)(2,1)S(1)}, bf16[1,64,4096]{2,1,0:T(8,128)(2,1)S(1)}, u32[]{:S(2)}, u32[]{:S(2)}) %collective-permute-start.2) | collective-permute-done | bytes 524320 | tf_op jit(solution)/shard_map/ppermute | solution.py:11
  60.7 1.3 multiply_convert_fusion.1
  63.1 0.5 convolution_bitcast_fusion.4
  63.6 0.8 slice.202
  64.4 1.3 collective-permute-start.3
  65.7 0.7 pad_maximum_fusion.14
  66.4 0.7 fusion.17
  67.1 0.7 pad_maximum_fusion.13
  67.9 27.3 %all-reduce.2 = (f32[2,256]{1,0:T(2,128)S(1)}, f32[2,128]{1,0:T(2,128)S(1)}) all-reduce(f32[2,256]{1,0:T(2,128)S(1)} %pad_maximum_fusion.15, f32[2,128]{1,0:T(2,128)S(1)} %pad_maximum_fusion.16), channel_id=1, replica_groups=mesh['corner'=16,'tm'=16] {'corner'}, use_global_device_ids=true, to_apply=%region_4.0 | all-reduce | flops 768 | bytes 6144 | tf_op jit(solution)/shard_map/psum | solution.py:134
  95.2 43.6 %all-reduce = (f32[2,256]{1,0:T(2,128)S(1)}, f32[2,128]{1,0:T(2,128)S(1)}) all-reduce(f32[2,256]{1,0:T(2,128)S(1)} %get-tuple-element.11, f32[2,128]{1,0:T(2,128)S(1)} %get-tuple-element.12), channel_id=1, replica_groups=mesh['corner'=16,'tm'=16] {'tm'}, use_global_device_ids=true, to_apply=%region_5.0 | all-reduce | flops 768 | bytes 6144 | tf_op jit(solution)/shard_map/psum | solution.py:133
  138.8 0.6 broadcast_multiply_fusion.3
  139.4 0.6 broadcast_multiply_fusion.2
  140.0 52.6 %all-reduce.9.cloned.1.call-done = (f32[2,256,128]{2,1,0:T(8,128)}, f32[2,128,128]{2,1,0:T(8,128)}) async-done(((f32[2,256,128]{2,1,0:T(8,128)}, f32[2,128,128]{2,1,0:T(8,128)}), (f32[2,256,128]{2,1,0:T(8,128)}, f32[2,128,128]{2,1,0:T(8,128)})) %all-reduce.9.cloned.1.call-update) | async-done | bytes 393232 | tf_op jit(solution)/shard_map/psum | solution.py:134
  192.6 1.0 fusion.21
  193.6 165.9 %all-reduce.7.cloned.1.call-done = (f32[2,256,128]{2,1,0:T(8,128)}, f32[2,128,128]{2,1,0:T(8,128)}) async-done(((f32[2,256,128]{2,1,0:T(8,128)}, f32[2,128,128]{2,1,0:T(8,128)}), (f32[2,256,128]{2,1,0:T(8,128)}, f32[2,128,128]{2,1,0:T(8,128)})) %all-reduce.7.cloned.1.call-update) | async-done | bytes 393232 | tf_op jit(solution)/shard_map/psum | solution.py:133
  359.5 1.7 broadcast_multiply_fusion
  361.2 1.6 broadcast_multiply_fusion.1
  (29 shorter events, 3.9 us)
Async XLA Ops:
  7.2 185.4 %all-reduce.9.cloned.1.call-start = ((), (), s32[]{:S(2)}) async-start(), calls=%async_computation.1 | async-start | bytes 786432 | tf_op jit(solution)/shard_map/psum | solution.py:134
  7.2 16.4 %collective-permute-start = (bf16[1,64,4096]{2,1,0:T(8,128)(2,1)}, bf16[1,64,4096]{2,1,0:T(8,128)(2,1)S(1)}, u32[]{:S(2)}, u32[]{:S(2)}) collective-permute-start(bf16[1,64,4096]{2,1,0:T(8,128)(2,1)} %param.7), channel_id=1, source_target_pairs={{0,1},{1,2},{2,3},{3,4},{4,5},{5,6},{6,7},{7,8},{8,9},{9,10},{10,1... | collective-permute-start | bytes 1572872 | tf_op jit(solution)/shard_map/ppermute | solution.py:11
  25.4 0.9 copy-start.4
  26.3 1.0 copy-start.2
  26.3 6.7 %copy-start.1 = (bf16[1,64,4096]{2,1,0:T(8,128)(2,1)S(1)}, bf16[1,64,4096]{2,1,0:T(8,128)(2,1)}, u32[]{:S(2)}) copy-start(bf16[1,64,4096]{2,1,0:T(8,128)(2,1)} %param.13) | copy-start | bytes 1572868
  27.3 16.0 %copy-start.3 = (bf16[2,256,128]{2,1,0:T(8,128)(2,1)S(1)}, bf16[2,256,128]{2,1,0:T(8,128)(2,1)}, u32[]{:S(2)}) copy-start(bf16[2,256,128]{2,1,0:T(8,128)(2,1)} %param.8) | copy-start | bytes 393220
  27.4 15.9 %collective-permute-start.1 = (bf16[1,64,4096]{2,1,0:T(8,128)(2,1)S(1)}, bf16[1,64,4096]{2,1,0:T(8,128)(2,1)S(1)}, u32[]{:S(2)}, u32[]{:S(2)}) collective-permute-start(bf16[1,64,4096]{2,1,0:T(8,128)(2,1)S(1)} %fusion.26), channel_id=1, source_target_pairs={{0,2},{1,3},{2,4},{3,5},{4,6},{5,7},{6,8},{7,9},{8,10},{9,11},{10,... | collective-permute-start | bytes 1572872 | tf_op jit(solution)/shard_map/ppermute | solution.py:11
  46.0 14.5 %collective-permute-start.2 = (bf16[1,64,4096]{2,1,0:T(8,128)(2,1)S(1)}, bf16[1,64,4096]{2,1,0:T(8,128)(2,1)S(1)}, u32[]{:S(2)}, u32[]{:S(2)}) collective-permute-start(bf16[1,64,4096]{2,1,0:T(8,128)(2,1)S(1)} %slice.203), channel_id=1, source_target_pairs={{2,0},{3,1},{4,2},{5,3},{6,4},{7,5},{8,6},{9,7},{10,8},{11,9},{12,... | collective-permute-start | bytes 1572872 | tf_op jit(solution)/shard_map/ppermute | solution.py:11
  50.0 10.5 %copy-start = (bf16[1,64,4096]{2,1,0:T(8,128)(2,1)S(1)}, bf16[1,64,4096]{2,1,0:T(8,128)(2,1)}, u32[]{:S(2)}) copy-start(bf16[1,64,4096]{2,1,0:T(8,128)(2,1)} %param.12) | copy-start | bytes 1572868
  64.4 128.2 %collective-permute-start.3 = (bf16[1,64,4096]{2,1,0:T(8,128)(2,1)}, bf16[1,64,4096]{2,1,0:T(8,128)(2,1)S(1)}, u32[]{:S(2)}, u32[]{:S(2)}) collective-permute-start(bf16[1,64,4096]{2,1,0:T(8,128)(2,1)} %slice.202), channel_id=1, source_target_pairs={{1,0},{2,1},{3,2},{4,3},{5,4},{6,5},{7,6},{8,7},{9,8},{10,9},{11,1... | collective-permute-start | bytes 1572872 | tf_op jit(solution)/shard_map/ppermute | solution.py:11
  67.9 291.6 %all-reduce.7.cloned.1.call-start = ((), (), s32[]{:S(2)}) async-start(), calls=%async_computation | async-start | bytes 786432 | tf_op jit(solution)/shard_map/psum | solution.py:133
Sparse Core Ops, SparseCore 0:
  68.0 124.5 all-reduce.8
  195.5 163.9 all-reduce.6
